TPU v7x, 128 devices: a whole 4x4x4 slice. The times are simulated.
128 devices in a mesh: gx: 8 (over z, y_lo), gy: 16 (over x, y_hi, core).
Axes of the slice: x: 4, y: 4 (y_hi: 2, y_lo: 2; y = y_hi * 2 + y_lo), z: 4, core: 2. Of those that a mesh axis runs over, the one named last changes fastest.
Arguments:
- velocity: float32 [3, 16, 1024, 2048], P(None, None, 'gx', 'gy'), may hold values from -6 to 6
- metric_first: float32 [2048], P('gy'), may hold values from 0.5 to 2
- metric_curve: float32 [2048], P('gy'), may hold values from -1 to 1
Outputs:
- tendency: float32 [3, 16, 1024, 2048], P(None, None, 'gx', 'gy')
All inputs are finite; a program needn't handle non-finite values.
Results may differ from a plain program's by a relative error of at most 0.0003.
Values sent between devices are 32-bit elements; how exact they have to be, the bound alone decides.
No kernel may reach another device: no remote copies, remote signals or barrier semaphores. Data moves between devices by JAX's collectives and lax.ppermute only.
A program may use at most 192 MiB of HBM per device.

v0:
```python
import functools

import jax
import jax.numpy as jnp
import numpy as np
from jax import lax
from jax.experimental import pallas as pl
from jax.experimental.pallas import tpu as pltpu
from jax.sharding import PartitionSpec as P

VISCOSITY = 0.1
F32 = jnp.float32
BF16 = jnp.bfloat16
GROUP = 8
KINDS = 3
EDGES = 2 * KINDS * GROUP


def coefficients(total, order, walls):
    alpha = 1.0 / 3.0 if order == 0 else 2.0 / 11.0
    lower = np.full(total, alpha)
    upper = np.full(total, alpha)
    lower[0] = 0.0
    upper[total - 1] = 0.0
    if walls:
        end = 2.0 if order == 0 else 0.0
        near = 0.25 if order == 0 else 0.1
        upper[0] = end
        lower[total - 1] = end
        for row in (1, total - 2):
            lower[row] = near
            upper[row] = near
    return lower, upper


def stencil_matrix(total, order, walls):
    matrix = np.zeros((total, total))
    if order == 0:
        taps = {1: 7.0 / 9.0, -1: -7.0 / 9.0, 2: 1.0 / 36.0, -2: -1.0 / 36.0}
    else:
        near, far = 12.0 / 11.0, 3.0 / 44.0
        taps = {0: -2.0 * (near + far), 1: near, -1: near, 2: far, -2: far}
    for offset, value in taps.items():
        rows = np.arange(max(0, -offset), total - max(0, offset))
        matrix[rows, rows + offset] = value
    if walls:
        matrix[[0, 1, -2, -1]] = 0.0
        if order == 0:
            matrix[0, :3] = [-2.5, 2.0, 0.5]
            matrix[1, :3] = [-0.75, 0.0, 0.75]
            matrix[-2, -3:] = [-0.75, 0.0, 0.75]
            matrix[-1, -3:] = [-0.5, -2.0, 2.5]
        else:
            matrix[0, :4] = [2.0, -5.0, 4.0, -1.0]
            matrix[1, :3] = [1.2, -2.4, 1.2]
            matrix[-2, -3:] = [1.2, -2.4, 1.2]
            matrix[-1, -4:] = [-1.0, 4.0, -5.0, 2.0]
    return matrix


class Inverse:
    def __init__(self, lower, upper):
        total = len(lower)
        self.down = np.zeros(total + 1)
        self.up = np.zeros(total + 1)
        low = np.zeros(total + 1)
        for i in range(total - 1, -1, -1):
            low[i] = lower[i] / (1.0 - upper[i] * low[i + 1])
        high = np.zeros(total + 1)
        for i in range(total):
            high[i] = upper[i] / (1.0 - lower[i] * high[i - 1])
        self.down[:total] = -low[:total]
        self.up[:total] = -high[:total]
        self.diagonal = np.array(
            [1.0 / (1.0 - lower[i] * high[i - 1] - upper[i] * low[i + 1]) for i in range(total)]
        )

    def column(self, j, first, last):
        values = np.zeros(last - first)
        value = self.diagonal[j]
        if first <= j < last:
            values[j - first] = value
        for i in range(j + 1, last):
            value = value * self.down[i]
            if i >= first:
                values[i - first] = value
        value = self.diagonal[j]
        for i in range(j - 1, first - 1, -1):
            value = value * self.up[i]
            if i < last:
                values[i - first] = value
        return values


def block_operator(total, order, walls, start, rows):
    lower, upper = coefficients(total, order, walls)
    inverse = Inverse(lower, upper)
    stencil = stencil_matrix(total, order, walls)
    stop = start + rows
    first, last = max(0, start - 2), min(total, stop + 2)
    columns = np.stack([inverse.column(j, start, stop) for j in range(first, last)], axis=1)
    own = columns @ stencil[first:last, start:stop]
    from_low = np.zeros((KINDS, rows))
    from_high = np.zeros((KINDS, rows))
    to_high = np.zeros(rows)
    to_low = np.zeros(rows)
    if start > 0:
        weight = np.cumprod(inverse.down[start:stop])
        from_low[1 + order] = weight
        beyond = inverse.diagonal[start + 1] / weight[1]
        gap = inverse.diagonal[start + 1] * inverse.up[start] - weight[0] * beyond
        from_low[0, 0] = gap * stencil[start + 1, start - 1]
        row = row_of(lower, upper, start, start, stop)
        weight = np.array([inverse.up[start - 1], inverse.up[start - 1] * inverse.up[start - 2]])
        q = np.concatenate(
            [
                [inverse.diagonal[start - 2] / weight[1], inverse.diagonal[start - 1] / weight[0]],
                row,
                row_of(lower, upper, start, stop, min(total, stop + 2)),
            ]
        )
        to_low = q @ stencil[start - 2 : min(total, stop + 2), start:stop]
    if stop < total:
        weight = np.cumprod(inverse.up[start:stop][::-1])[::-1]
        from_high[1 + order] = weight
        beyond = inverse.diagonal[stop - 2] / weight[-2]
        gap = inverse.diagonal[stop - 2] * inverse.down[stop - 1] - weight[-1] * beyond
        from_high[0, -1] = gap * stencil[stop - 2, stop]
        row = row_of(lower, upper, stop - 1, max(0, start - 2), stop)
        weight = np.array([inverse.down[stop], inverse.down[stop] * inverse.down[stop + 1]])
        v = np.concatenate(
            [row, [inverse.diagonal[stop] / weight[0], inverse.diagonal[stop + 1] / weight[1]]]
        )
        to_high = v @ stencil[max(0, start - 2) : stop + 2, start:stop]
    return own, from_low, from_high, to_high, to_low


def row_of(lower, upper, i, first, last):
    turned = Inverse(np.append(0.0, upper[:-1]), np.append(lower[1:], 0.0))
    return turned.column(i, first, last)


def line_tables(total, walls, start, rows, even):
    orders = [block_operator(total, order, walls, start, rows) for order in (0, 1)]
    own = np.stack([item[0] for item in orders])
    low = np.stack([item[1] for item in orders])
    high = np.stack([item[2] for item in orders])
    edge_high = np.zeros(rows)
    edge_high[-1] = 1.0
    edge_low = np.zeros(rows)
    edge_low[0] = 1.0
    to_high = np.stack([edge_high, orders[0][3], orders[1][3]])
    to_low = np.stack([edge_low, orders[0][4], orders[1][4]])
    received = np.concatenate([high, low] if even else [low, high], axis=1)
    sent = np.concatenate([to_high, to_low] if even else [to_low, to_high])
    return own, np.repeat(received, GROUP, axis=1), np.repeat(sent, GROUP, axis=0)


def halves(values):
    high = values.astype(BF16)
    low = (values - high.astype(np.float64)).astype(BF16)
    return high, low


def split(values):
    high = values.astype(BF16)
    low = (values - high.astype(F32)).astype(BF16)
    return high, low


def sum_rows(stacked, concatenate):
    half = EDGES // 2
    return concatenate([stacked[GROUP:half], stacked[half + GROUP :]])


def x_tables(rows):
    sums, mains = [], []
    for even in (True, False):
        own, received, sent = line_tables(5 * rows, False, 2 * rows, rows, even)
        scale = np.array([-1.0, VISCOSITY])[:, None, None]
        high, low = halves((own * scale).reshape(2 * rows, rows))
        edge, rest = halves((received * scale).transpose(1, 0, 2).reshape(EDGES, 2 * rows))
        edge = np.concatenate([edge, edge, sum_rows(rest, np.concatenate)]).T
        mains.append(np.concatenate([high, high, low, edge], axis=1))
        high, low = halves(sent)
        sums.append(
            np.concatenate(
                [np.concatenate([high, high], axis=1), np.concatenate([low, 0 * low], axis=1)]
            )
        )
    return np.stack(sums), np.stack(mains)


def y_tables(parts, rows):
    sums, mains, edges = [], [], []
    for part, even in ((0, True), (2, True), (3, False), (parts - 1, False)):
        own, received, sent = line_tables(parts * rows, True, part * rows, rows, even)
        mains.append(np.concatenate([own[0].T, own[1].T], axis=1))
        edges.append(np.concatenate([received[0], received[1]], axis=1))
        if part in (0, parts - 1):
            continue
        high, low = halves(sent)
        pad = np.zeros((rows // 2 - EDGES, 2 * rows), high.dtype)
        sums.append(
            np.concatenate(
                [
                    np.concatenate([high, high], axis=1),
                    pad,
                    np.concatenate([low, 0 * low], axis=1),
                    pad,
                ]
            ).T
        )
    return np.stack(sums), np.stack(mains).astype(np.float32), np.stack(edges).astype(np.float32)


def edge_kernel(
    chunk,
    field_hbm,
    x_hbm,
    y_hbm,
    x_main_hbm,
    y_main_hbm,
    y_edge_hbm,
    x1_ref,
    x2_ref,
    y1_ref,
    y2_ref,
    field_ref,
    x_main_ref,
    y_main_ref,
    y_edge_ref,
    x_ref,
    y_ref,
    x_acc,
    y_acc,
    field_sems,
    table_sems,
):
    parts, planes, rows, _ = field_ref.shape
    x_odd = lax.axis_index("gx") % 2
    y_index = lax.axis_index("gy")
    y_odd = y_index % 2
    last = lax.axis_size("gy") - 1
    kind = jnp.where(y_index == 0, 0, jnp.where(y_index == last, 3, 1 + y_odd))

    def fetch(i):
        place = pl.ds(i * chunk, chunk)
        return pltpu.make_async_copy(
            field_hbm.at[:, place], field_ref.at[:, place], field_sems.at[i]
        )

    sums = [
        pltpu.make_async_copy(x_hbm.at[x_odd], x_ref, table_sems.at[3]),
        pltpu.make_async_copy(y_hbm.at[y_odd], y_ref, table_sems.at[4]),
    ]
    for copy in sums:
        copy.start()
    steps = planes // chunk
    for i in range(steps):
        fetch(i).start()
    tables = [
        pltpu.make_async_copy(x_main_hbm.at[x_odd], x_main_ref, table_sems.at[0]),
        pltpu.make_async_copy(y_main_hbm.at[kind], y_main_ref, table_sems.at[1]),
        pltpu.make_async_copy(y_edge_hbm.at[kind], y_edge_ref, table_sems.at[2]),
    ]
    for copy in tables:
        copy.start()

    x_row = lax.broadcasted_iota(jnp.int32, (EDGES, rows), 0) % GROUP
    y_lane = lax.broadcasted_iota(jnp.int32, (rows, rows), 1) % GROUP
    half = EDGES // 2
    for copy in sums:
        copy.wait()

    def body(i, carry):
        fetch(i).wait()
        base = lax.rem(i * chunk, GROUP)
        for part in range(parts):
            for z in range(chunk):
                high, low = split(field_ref[part, i * chunk + z])
                place = base + z
                sums = jnp.dot(
                    x_ref[...],
                    jnp.concatenate([high, low], axis=0),
                    preferred_element_type=F32,
                )
                sums = sums[:EDGES] + sums[EDGES:]
                x_acc[part] = jnp.where(x_row == place, sums, x_acc[part])
                sums = jnp.dot(
                    jnp.concatenate([high, low], axis=1),
                    y_ref[...],
                    preferred_element_type=F32,
                )
                y_acc[part] = jnp.where(y_lane == place, sums, y_acc[part])

        @pl.when(base + chunk == GROUP)
        def _():
            start = pl.multiple_of(i * chunk + chunk - GROUP, GROUP)
            target = pl.ds(start, GROUP)
            for part in range(parts):
                values = x_acc[part]
                turned = y_acc[part].T
                turned = turned[:EDGES] + turned[rows // 2 : rows // 2 + EDGES]
                for kind in range(KINDS):
                    near = slice(kind * GROUP, (kind + 1) * GROUP)
                    far = slice(half + kind * GROUP, half + (kind + 1) * GROUP)
                    x1_ref[kind, part, target] = values[near]
                    x2_ref[kind, part, target] = values[far]
                    y1_ref[kind, part, target] = turned[near]
                    y2_ref[kind, part, target] = turned[far]

        return carry

    lax.fori_loop(0, steps, body, 0)
    for copy in tables:
        copy.wait()


def stack_edges(first_ref, second_ref, part, group):
    place = pl.ds(pl.multiple_of(group * GROUP, GROUP), GROUP)
    values = jnp.concatenate(
        [ref[kind, part, place] for ref in (first_ref, second_ref) for kind in range(KINDS)]
    )
    high = values.astype(BF16).astype(F32)
    return jnp.concatenate([high, values - high, sum_rows(high, jnp.concatenate)])


def wall_normal_kernel(
    depth, field_ref, first_ref, second_ref, main_ref, edge_ref, m_ref, curve_ref, out_ref, w_ref
):
    parts, planes, rows, _ = field_ref.shape
    m = m_ref[...]
    curve = curve_ref[...]

    def scaled(table):
        one = table[:, :rows]
        two = table[:, rows:]
        return jnp.concatenate([one * -m, VISCOSITY * (two * (m * m) + one * curve)], axis=1)

    high, low = split(scaled(main_ref[...]))
    edge, rest = split(scaled(edge_ref[...]))
    rest = sum_rows(rest, jnp.concatenate)
    w_ref[...] = jnp.concatenate([high, high, low, edge, edge, rest])
    lane = lax.broadcasted_iota(jnp.int32, (rows, rows), 1) % GROUP

    def body(i, carry):
        start = i * depth
        base = lax.rem(start, GROUP)
        blocks = []
        for part in range(parts):
            edges = stack_edges(first_ref, second_ref, part, start // GROUP).T
            for z in range(depth):
                high, low = split(field_ref[part, start + z])
                edge = jnp.where(lane == base + z, edges, 0.0).astype(BF16)
                blocks.append(jnp.concatenate([high, low, high, edge], axis=1))
        sums = jnp.dot(jnp.concatenate(blocks), w_ref[...], preferred_element_type=F32)
        for part in range(parts):
            for z in range(depth):
                piece = sums[(part * depth + z) * rows : (part * depth + z + 1) * rows]
                normal = field_ref[1, start + z]
                out_ref[part, start + z] = normal * piece[:, :rows] + piece[:, rows:]
        return carry

    lax.fori_loop(0, planes // depth, body, 0)


def streamwise_kernel(depth, field_ref, first_ref, second_ref, main_ref, add_ref, out_ref):
    parts, _, rows, _ = field_ref.shape
    start = pl.program_id(0) * depth
    base = lax.rem(start, GROUP)
    row = lax.broadcasted_iota(jnp.int32, (rows, rows), 0) % GROUP
    for part in range(parts):
        edges = stack_edges(first_ref, second_ref, part, start // GROUP)
        blocks = []
        for z in range(depth):
            high, low = split(field_ref[part, start + z])
            edge = jnp.where(row == base + z, edges, 0.0).astype(BF16)
            blocks.append(jnp.concatenate([high, low, high, edge]))
        sums = jnp.dot(
            main_ref[...], jnp.concatenate(blocks, axis=1), preferred_element_type=F32
        )
        for z in range(depth):
            piece = sums[:, z * rows : (z + 1) * rows]
            out_ref[part, z] = (
                field_ref[0, start + z] * piece[:rows] + piece[rows:] + add_ref[part, start + z]
            )


def exchange(first, second, axis, count, periodic):
    pairs = [(i, i + 1) for i in range(0, count, 2)]
    first = lax.ppermute(first, axis, [p for a, b in pairs for p in ((a, b), (b, a))])
    pairs = [(i, (i + 1) % count) for i in range(1, count if periodic else count - 1, 2)]
    second = lax.ppermute(second, axis, [p for a, b in pairs for p in ((a, b), (b, a))])
    return first, second


CHUNK = 2
DEPTH = 8


def on_device(x_parts, y_parts, velocity, metric_first, metric_curve):
    parts, planes, rows, _ = velocity.shape
    x_sums, x_main = x_tables(rows)
    y_sums, y_main, y_edge = y_tables(y_parts, rows)
    vmem = pl.BlockSpec(memory_space=pltpu.VMEM)
    outside = pl.BlockSpec(memory_space=pltpu.HBM)
    edge_shape = jax.ShapeDtypeStruct((KINDS, parts, planes, rows), F32)

    def on_chip(shape, dtype):
        return pltpu.VMEM(shape, dtype)

    in_specs = [outside] * 6
    x1, x2, y1, y2, field, x_main, y_main, y_edge = pl.pallas_call(
        functools.partial(edge_kernel, CHUNK),
        out_shape=[edge_shape] * 4
        + [
            on_chip(velocity.shape, F32),
            on_chip(x_main.shape[1:], BF16),
            on_chip(y_main.shape[1:], F32),
            on_chip(y_edge.shape[1:], F32),
        ],
        in_specs=in_specs,
        out_specs=[vmem] * 8,
        scratch_shapes=[
            pltpu.VMEM(x_sums.shape[1:], BF16),
            pltpu.VMEM(y_sums.shape[1:], BF16),
            pltpu.VMEM((parts, EDGES, rows), F32),
            pltpu.VMEM((parts, rows, rows), F32),
            pltpu.SemaphoreType.DMA((planes // CHUNK,)),
            pltpu.SemaphoreType.DMA((5,)),
        ],
        compiler_params=pltpu.CompilerParams(vmem_limit_bytes=16 << 20),
        name="edges",
    )(*[
        pltpu.with_memory_space_constraint(item, pltpu.HBM)
        for item in (velocity, x_sums, y_sums, x_main, y_main, y_edge)
    ])

    y1, y2 = exchange(y1, y2, "gy", y_parts, False)
    x1, x2 = exchange(x1, x2, "gx", x_parts, True)

    params = pltpu.CompilerParams(vmem_limit_bytes=16 << 20)
    partial = pl.pallas_call(
        functools.partial(wall_normal_kernel, DEPTH),
        out_shape=on_chip(velocity.shape, F32),
        in_specs=[vmem] * 7,
        out_specs=vmem,
        scratch_shapes=[pltpu.VMEM((4 * rows, 2 * rows), BF16)],
        compiler_params=params,
        name="wall_normal",
    )(field, y1, y2, y_main, y_edge, metric_first[None], metric_curve[None])

    return pl.pallas_call(
        functools.partial(streamwise_kernel, DEPTH),
        out_shape=jax.ShapeDtypeStruct(velocity.shape, F32),
        grid=(planes // DEPTH,),
        in_specs=[vmem] * 5,
        out_specs=pl.BlockSpec((parts, DEPTH, rows, rows), lambda i: (0, i, 0, 0)),
        compiler_params=params,
        name="streamwise",
    )(field, x1, x2, x_main, partial)


def solution(mesh):
    placed = (P(None, None, "gx", "gy"), P("gy"), P("gy"))
    return jax.shard_map(
        functools.partial(on_device, mesh.shape["gx"], mesh.shape["gy"]),
        mesh=mesh,
        in_specs=placed,
        out_specs=P(None, None, "gx", "gy"),
        check_vma=False,
    )
```

profile of v0, /device:TPU:2, one launch (start us, length us, event | category | flops | bytes accessed | tf_op | source)
XLA Modules:
  0.0 23.3 jit_solution(1375908326504639480)
XLA Ops:
  0.0 0.0 copy-start.1
  0.0 0.0 copy-start
  0.0 4.6 %edges.1 = (f32[3,3,16,128]{3,2,1,0:T(8,128)S(1)}, f32[3,3,16,128]{3,2,1,0:T(8,128)S(1)}, f32[3,3,16,128]{3,2,1,0:T(8,128)S(1)}, f32[3,3,16,128]{3,2,1,0:T(8,128...) custom-call(f32[3,16,128,128]{3,2,1,0:T(8,128)} %field_hbm.1, ...), custom_call_target="tpu_custom_call" | custom-call | tf_op jit(solution)/shard_map/edges/pallas_call | solution.py:414
  4.6 0.1 collective-permute-start.2
  4.7 5.2 %collective-permute-start.3 = (f32[3,3,16,128]{3,2,1,0:T(8,128)S(1)}, f32[3,3,16,128]{3,2,1,0:T(8,128)S(1)}, u32[]{:S(2)}, u32[]{:S(2)}) collective-permute-start(f32[3,3,16,128]{3,2,1,0:T(8,128)S(1)} %get-tuple-element.18), channel_id=1, source_target_pairs={{1,2},{2,1},{3,4},{4,3},{5,6},{6,5},{7,8},{8,7},{9,10},{10,9},{11,... | collective-permute-start | bytes 221192 | tf_op jit(solution)/shard_map/ppermute | solution.py:394
  9.9 0.8 %collective-permute-start = (f32[3,3,16,128]{3,2,1,0:T(8,128)S(1)}, f32[3,3,16,128]{3,2,1,0:T(8,128)S(1)}, u32[]{:S(2)}, u32[]{:S(2)}) collective-permute-start(f32[3,3,16,128]{3,2,1,0:T(8,128)S(1)} %get-tuple-element.14), channel_id=1, source_target_pairs={{0,16},{16,0},{32,48},{48,32},{64,80},{80,64},{96,112},{112,96},{1... | collective-permute-start | bytes 221192 | tf_op jit(solution)/shard_map/ppermute | solution.py:392
  10.6 4.8 %collective-permute-start.1 = (f32[3,3,16,128]{3,2,1,0:T(8,128)S(1)}, f32[3,3,16,128]{3,2,1,0:T(8,128)S(1)}, u32[]{:S(2)}, u32[]{:S(2)}) collective-permute-start(f32[3,3,16,128]{3,2,1,0:T(8,128)S(1)} %get-tuple-element.15), channel_id=1, source_target_pairs={{16,32},{32,16},{48,64},{64,48},{80,96},{96,80},{112,0},{0,112},{1... | collective-permute-start | bytes 221192 | tf_op jit(solution)/shard_map/ppermute | solution.py:394
  15.4 0.0 collective-permute-done.2.first_ref
  15.5 0.0 collective-permute-done.3.second_ref
  15.5 0.0 copy-done.1
  15.5 0.0 copy-done
  15.5 2.1 %wall_normal.1.add_ref = f32[3,16,128,128]{3,2,1,0:T(8,128)S(1)} custom-call(f32[3,16,128,128]{3,2,1,0:T(8,128)S(1)} %get-tuple-element.13.field_ref, f32[3,3,16,128]{3,2,1,0:T(8,128)S(1)} %collective-permute-done.2.first_ref, f32[3,3,16,128]{3,2,1,0:T(8,128)S(1)} %collective-permute-done.3.second_ref, f32[128,256]{1,0:T(8,128)S(1)} %get-tuple-element.19.main_ref, ...), custom_call_target="tpu_custom_call" | custom-call | tf_op jit(solution)/shard_map/wall_normal/pallas_call | solution.py:444
  17.6 0.0 collective-permute-done.first_ref
  17.6 2.4 %collective-permute-done.1.second_ref = f32[3,3,16,128]{3,2,1,0:T(8,128)S(1)} collective-permute-done((f32[3,3,16,128]{3,2,1,0:T(8,128)S(1)}, f32[3,3,16,128]{3,2,1,0:T(8,128)S(1)}, u32[]{:S(2)}, u32[]{:S(2)}) %collective-permute-start.1) | collective-permute-done | bytes 73760 | tf_op jit(solution)/shard_map/ppermute | solution.py:394
  20.0 3.3 %streamwise.1 = f32[3,16,128,128]{3,2,1,0:T(8,128)} custom-call(f32[3,16,128,128]{3,2,1,0:T(8,128)S(1)} %get-tuple-element.13.field_ref, f32[3,3,16,128]{3,2,1,0:T(8,128)S(1)} %collective-permute-done.first_ref, f32[3,3,16,128]{3,2,1,0:T(8,128)S(1)} %collective-permute-done.1.second_ref, bf16[256,512]{1,0:T(8,128)(2,1)S(1)} %get-tuple-element.16.main_ref, ...), custom_call_target="tpu_custom_call" | custom-call | tf_op jit(solution)/shard_map/streamwise/pallas_call | solution.py:454
Async XLA Ops:
  0.0 15.5 %copy-start.1 = (f32[128]{0:T(128)S(1)}, f32[128]{0:T(128)}, u32[]{:S(2)}) copy-start(f32[128]{0:T(128)} %param.10) | copy-start | bytes 1540
  0.0 15.5 %copy-start = (f32[128]{0:T(128)S(1)}, f32[128]{0:T(128)}, u32[]{:S(2)}) copy-start(f32[128]{0:T(128)} %param.9) | copy-start | bytes 1540
  4.6 10.8 %collective-permute-start.2 = (f32[3,3,16,128]{3,2,1,0:T(8,128)S(1)}, f32[3,3,16,128]{3,2,1,0:T(8,128)S(1)}, u32[]{:S(2)}, u32[]{:S(2)}) collective-permute-start(f32[3,3,16,128]{3,2,1,0:T(8,128)S(1)} %get-tuple-element.17), channel_id=1, source_target_pairs={{0,1},{1,0},{2,3},{3,2},{4,5},{5,4},{6,7},{7,6},{8,9},{9,8},{10,11... | collective-permute-start | bytes 221192 | tf_op jit(solution)/shard_map/ppermute | solution.py:392
  4.7 10.8 %collective-permute-start.3 = (f32[3,3,16,128]{3,2,1,0:T(8,128)S(1)}, f32[3,3,16,128]{3,2,1,0:T(8,128)S(1)}, u32[]{:S(2)}, u32[]{:S(2)}) collective-permute-start(f32[3,3,16,128]{3,2,1,0:T(8,128)S(1)} %get-tuple-element.18), channel_id=1, source_target_pairs={{1,2},{2,1},{3,4},{4,3},{5,6},{6,5},{7,8},{8,7},{9,10},{10,9},{11,... | collective-permute-start | bytes 221192 | tf_op jit(solution)/shard_map/ppermute | solution.py:394
  9.9 7.7 %collective-permute-start = (f32[3,3,16,128]{3,2,1,0:T(8,128)S(1)}, f32[3,3,16,128]{3,2,1,0:T(8,128)S(1)}, u32[]{:S(2)}, u32[]{:S(2)}) collective-permute-start(f32[3,3,16,128]{3,2,1,0:T(8,128)S(1)} %get-tuple-element.14), channel_id=1, source_target_pairs={{0,16},{16,0},{32,48},{48,32},{64,80},{80,64},{96,112},{112,96},{1... | collective-permute-start | bytes 221192 | tf_op jit(solution)/shard_map/ppermute | solution.py:392
  10.6 9.4 %collective-permute-start.1 = (f32[3,3,16,128]{3,2,1,0:T(8,128)S(1)}, f32[3,3,16,128]{3,2,1,0:T(8,128)S(1)}, u32[]{:S(2)}, u32[]{:S(2)}) collective-permute-start(f32[3,3,16,128]{3,2,1,0:T(8,128)S(1)} %get-tuple-element.15), channel_id=1, source_target_pairs={{16,32},{32,16},{48,64},{64,48},{80,96},{96,80},{112,0},{0,112},{1... | collective-permute-start | bytes 221192 | tf_op jit(solution)/shard_map/ppermute | solution.py:394
where the time goes:
time: 23.4 us; the launch traced here: 23.3 us
  starting transfers between devices  10.8 us (46%)
  Pallas kernels  9.94 us (42%)
  waiting for transfers between devices  2.45 us (10%)
    ppermute x2, starting transfers between devices, exchange(): lax.ppermute(second, axis, [p for a, b in pairs for p in ((a, b), (b, a))])  9.99 us
    pallas_call x1, Pallas kernels, on_device(): pl.pallas_call(functools.partial(edge_kernel, CHUNK), out_shape=[edge_sha...  4.59 us
    pallas_call x1, Pallas kernels, on_device(): pl.pallas_call(functools.partial(streamwise_kernel, DEPTH), out_shape=jax...  3.26 us
    ppermute x2, waiting for transfers between devices, exchange(): lax.ppermute(second, axis, [p for a, b in pairs for p in ((a, b), (b, a))])  2.44 us
    pallas_call x1, Pallas kernels, on_device(): pl.pallas_call(functools.partial(wall_normal_kernel, DEPTH), out_shape=on...  2.09 us
    ppermute x2, starting transfers between devices, exchange(): lax.ppermute(first, axis, [p for a, b in pairs for p in ((a, b), (b, a))])  0.84 us
  transfers between devices with their start and end apart: 4, of which 1 were waited for; matrix products, arithmetic and copies ran while one was open for 0% of the time, Pallas kernels for 9%

commit v1 on v0

--- a/solution.py
+++ b/solution.py
@@ -152,8 +152,7 @@
     to_high = np.stack([edge_high, orders[0][3], orders[1][3]])
     to_low = np.stack([edge_low, orders[0][4], orders[1][4]])
     received = np.concatenate([high, low] if even else [low, high], axis=1)
-    sent = np.concatenate([to_high, to_low] if even else [to_low, to_high])
-    return own, np.repeat(received, GROUP, axis=1), np.repeat(sent, GROUP, axis=0)
+    return own, np.repeat(received, GROUP, axis=1), np.concatenate([to_high, to_low])
 
 
 def halves(values):
@@ -174,7 +173,7 @@
 
 
 def x_tables(rows):
-    sums, mains = [], []
+    mains = []
     for even in (True, False):
         own, received, sent = line_tables(5 * rows, False, 2 * rows, rows, even)
         scale = np.array([-1.0, VISCOSITY])[:, None, None]
@@ -182,58 +181,42 @@
         edge, rest = halves((received * scale).transpose(1, 0, 2).reshape(EDGES, 2 * rows))
         edge = np.concatenate([edge, edge, sum_rows(rest, np.concatenate)]).T
         mains.append(np.concatenate([high, high, low, edge], axis=1))
-        high, low = halves(sent)
-        sums.append(
-            np.concatenate(
-                [np.concatenate([high, high], axis=1), np.concatenate([low, 0 * low], axis=1)]
-            )
-        )
-    return np.stack(sums), np.stack(mains)
+    sums = np.delete(sent, [0, KINDS], axis=0).astype(np.float32)
+    return np.repeat(sums[:, :, None], rows, axis=2), np.stack(mains)
 
 
 def y_tables(parts, rows):
-    sums, mains, edges = [], [], []
+    mains, edges = [], []
     for part, even in ((0, True), (2, True), (3, False), (parts - 1, False)):
         own, received, sent = line_tables(parts * rows, True, part * rows, rows, even)
         mains.append(np.concatenate([own[0].T, own[1].T], axis=1))
         edges.append(np.concatenate([received[0], received[1]], axis=1))
-        if part in (0, parts - 1):
-            continue
-        high, low = halves(sent)
-        pad = np.zeros((rows // 2 - EDGES, 2 * rows), high.dtype)
-        sums.append(
-            np.concatenate(
-                [
-                    np.concatenate([high, high], axis=1),
-                    pad,
-                    np.concatenate([low, 0 * low], axis=1),
-                    pad,
-                ]
-            ).T
-        )
-    return np.stack(sums), np.stack(mains).astype(np.float32), np.stack(edges).astype(np.float32)
-
-
-def edge_kernel(
+        if part == 2:
+            high, low = halves(np.repeat(sent, GROUP, axis=0))
+            pad = np.zeros((rows // 2 - EDGES, 2 * rows), high.dtype)
+            upper = np.concatenate([high, high], axis=1)
+            lower = np.concatenate([low, 0 * low], axis=1)
+            sums = np.concatenate([upper, pad, lower, pad]).T
+    return sums, np.stack(mains).astype(np.float32), np.stack(edges).astype(np.float32)
+
+
+def y_edge_kernel(
     chunk,
     field_hbm,
+    y_hbm,
     x_hbm,
-    y_hbm,
     x_main_hbm,
     y_main_hbm,
     y_edge_hbm,
-    x1_ref,
-    x2_ref,
     y1_ref,
     y2_ref,
     field_ref,
+    x_ref,
     x_main_ref,
     y_main_ref,
     y_edge_ref,
-    x_ref,
     y_ref,
-    x_acc,
-    y_acc,
+    acc,
     field_sems,
     table_sems,
 ):
@@ -243,78 +226,104 @@
     y_odd = y_index % 2
     last = lax.axis_size("gy") - 1
     kind = jnp.where(y_index == 0, 0, jnp.where(y_index == last, 3, 1 + y_odd))
-
-    def fetch(i):
+    sums = pltpu.make_async_copy(y_hbm, y_ref, table_sems.at[0])
+    sums.start()
+    fetches = []
+    for i in range(planes // chunk):
         place = pl.ds(i * chunk, chunk)
-        return pltpu.make_async_copy(
-            field_hbm.at[:, place], field_ref.at[:, place], field_sems.at[i]
+        fetches.append(
+            pltpu.make_async_copy(
+                field_hbm.at[:, place], field_ref.at[:, place], field_sems.at[i]
+            )
         )
-
-    sums = [
-        pltpu.make_async_copy(x_hbm.at[x_odd], x_ref, table_sems.at[3]),
-        pltpu.make_async_copy(y_hbm.at[y_odd], y_ref, table_sems.at[4]),
-    ]
-    for copy in sums:
-        copy.start()
-    steps = planes // chunk
-    for i in range(steps):
-        fetch(i).start()
+        fetches[-1].start()
     tables = [
-        pltpu.make_async_copy(x_main_hbm.at[x_odd], x_main_ref, table_sems.at[0]),
-        pltpu.make_async_copy(y_main_hbm.at[kind], y_main_ref, table_sems.at[1]),
-        pltpu.make_async_copy(y_edge_hbm.at[kind], y_edge_ref, table_sems.at[2]),
+        pltpu.make_async_copy(x_hbm, x_ref, table_sems.at[1]),
+        pltpu.make_async_copy(y_main_hbm.at[kind], y_main_ref, table_sems.at[2]),
+        pltpu.make_async_copy(y_edge_hbm.at[kind], y_edge_ref, table_sems.at[3]),
+        pltpu.make_async_copy(x_main_hbm.at[x_odd], x_main_ref, table_sems.at[4]),
     ]
     for copy in tables:
         copy.start()
-
-    x_row = lax.broadcasted_iota(jnp.int32, (EDGES, rows), 0) % GROUP
-    y_lane = lax.broadcasted_iota(jnp.int32, (rows, rows), 1) % GROUP
+    sums.wait()
+
+    lane = lax.broadcasted_iota(jnp.int32, (rows, rows), 1) % GROUP
     half = EDGES // 2
-    for copy in sums:
-        copy.wait()
-
-    def body(i, carry):
-        fetch(i).wait()
-        base = lax.rem(i * chunk, GROUP)
+    for i, fetch in enumerate(fetches):
+        fetch.wait()
+        blocks = []
         for part in range(parts):
+            for z in range(i * chunk, (i + 1) * chunk):
+                blocks.append(jnp.concatenate(split(field_ref[part, z]), axis=1))
+        middle = len(blocks) // 2
+        found = [
+            jnp.dot(jnp.concatenate(some), y_ref[...], preferred_element_type=F32)
+            for some in (blocks[:middle], blocks[middle:])
+        ]
+        base = i * chunk % GROUP
+        for part in range(parts):
+            value = None if base == 0 else acc[part]
             for z in range(chunk):
-                high, low = split(field_ref[part, i * chunk + z])
-                place = base + z
-                sums = jnp.dot(
-                    x_ref[...],
-                    jnp.concatenate([high, low], axis=0),
-                    preferred_element_type=F32,
-                )
-                sums = sums[:EDGES] + sums[EDGES:]
-                x_acc[part] = jnp.where(x_row == place, sums, x_acc[part])
-                sums = jnp.dot(
-                    jnp.concatenate([high, low], axis=1),
-                    y_ref[...],
-                    preferred_element_type=F32,
-                )
-                y_acc[part] = jnp.where(y_lane == place, sums, y_acc[part])
-
-        @pl.when(base + chunk == GROUP)
-        def _():
-            start = pl.multiple_of(i * chunk + chunk - GROUP, GROUP)
-            target = pl.ds(start, GROUP)
-            for part in range(parts):
-                values = x_acc[part]
-                turned = y_acc[part].T
-                turned = turned[:EDGES] + turned[rows // 2 : rows // 2 + EDGES]
-                for kind in range(KINDS):
-                    near = slice(kind * GROUP, (kind + 1) * GROUP)
-                    far = slice(half + kind * GROUP, half + (kind + 1) * GROUP)
-                    x1_ref[kind, part, target] = values[near]
-                    x2_ref[kind, part, target] = values[far]
-                    y1_ref[kind, part, target] = turned[near]
-                    y2_ref[kind, part, target] = turned[far]
-
-        return carry
-
-    lax.fori_loop(0, steps, body, 0)
+                side, place = divmod(part * chunk + z, middle)
+                piece = found[side][place * rows : (place + 1) * rows]
+                value = piece if value is None else jnp.where(lane == base + z, piece, value)
+            if base + chunk < GROUP:
+                acc[part] = value
+                continue
+            turned = value.T
+            turned = turned[:EDGES] + turned[rows // 2 : rows // 2 + EDGES]
+            to_high, to_low = turned[:half], turned[half:]
+            first = jnp.where(y_odd == 0, to_high, to_low)
+            second = jnp.where(y_odd == 0, to_low, to_high)
+            target = slice((i + 1) * chunk - GROUP, (i + 1) * chunk)
+            for kind in range(KINDS):
+                tile = slice(kind * GROUP, (kind + 1) * GROUP)
+                y1_ref[kind, part, target] = first[tile]
+                y2_ref[kind, part, target] = second[tile]
     for copy in tables:
         copy.wait()
+
+
+def x_edge_kernel(chunk, spans, field_ref, x_ref, x1_ref, x2_ref, acc):
+    parts, planes, rows, lanes = field_ref.shape
+    x_odd = lax.axis_index("gx") % 2
+
+    def body(i, carry):
+        part = i // (planes // chunk)
+        start = lax.rem(i, planes // chunk) * chunk
+        sums = [[None] * chunk for _ in spans]
+        for tile in range(0, rows, GROUP):
+            place = slice(tile, tile + GROUP)
+            cells = [field_ref[part, start + z, place] for z in range(chunk)]
+            for which, (first, last) in enumerate(spans):
+                if first <= tile < last:
+                    weight = x_ref[which, place]
+                    for z in range(chunk):
+                        term = weight * cells[z]
+                        old = sums[which][z]
+                        sums[which][z] = term if old is None else old + term
+        for z in range(chunk):
+            row = pl.ds(start + z, 1)
+            for which in range(4):
+                direction, order = divmod(which, 2)
+                acc[direction, 1 + order, part, row] = jnp.sum(
+                    sums[which][z], axis=0, keepdims=True
+                )
+            acc[0, 0, part, row] = field_ref[part, start + z, rows - 1 : rows]
+            acc[1, 0, part, row] = field_ref[part, start + z, 0:1]
+        return carry
+
+    lax.fori_loop(0, parts * planes // chunk, body, 0)
+    x1_ref[...] = acc[x_odd]
+    x2_ref[...] = acc[1 - x_odd]
+
+
+def spans_of(weights):
+    spans = []
+    for values in weights[:, :, 0]:
+        rows = np.flatnonzero(np.abs(values) >= np.finfo(np.float32).tiny)
+        spans.append((rows[0] // GROUP * GROUP, -(-(rows[-1] + 1) // GROUP) * GROUP))
+    return tuple((int(first), int(last)) for first, last in spans)
 
 
 def stack_edges(first_ref, second_ref, part, group):
@@ -327,7 +336,7 @@
 
 
 def wall_normal_kernel(
-    depth, field_ref, first_ref, second_ref, main_ref, edge_ref, m_ref, curve_ref, out_ref, w_ref
+    depth, field_ref, second_ref, first_ref, main_ref, edge_ref, m_ref, curve_ref, out_ref, w_ref
 ):
     parts, planes, rows, _ = field_ref.shape
     m = m_ref[...]
@@ -365,26 +374,35 @@
     lax.fori_loop(0, planes // depth, body, 0)
 
 
-def streamwise_kernel(depth, field_ref, first_ref, second_ref, main_ref, add_ref, out_ref):
-    parts, _, rows, _ = field_ref.shape
-    start = pl.program_id(0) * depth
-    base = lax.rem(start, GROUP)
+def streamwise_kernel(
+    depth, field_ref, second_ref, first_ref, main_ref, add_ref, out_hbm, out_ref, sems
+):
+    parts, planes, rows, _ = field_ref.shape
     row = lax.broadcasted_iota(jnp.int32, (rows, rows), 0) % GROUP
-    for part in range(parts):
-        edges = stack_edges(first_ref, second_ref, part, start // GROUP)
-        blocks = []
-        for z in range(depth):
-            high, low = split(field_ref[part, start + z])
-            edge = jnp.where(row == base + z, edges, 0.0).astype(BF16)
-            blocks.append(jnp.concatenate([high, low, high, edge]))
-        sums = jnp.dot(
-            main_ref[...], jnp.concatenate(blocks, axis=1), preferred_element_type=F32
-        )
-        for z in range(depth):
-            piece = sums[:, z * rows : (z + 1) * rows]
-            out_ref[part, z] = (
-                field_ref[0, start + z] * piece[:rows] + piece[rows:] + add_ref[part, start + z]
+    copies = []
+    for start in range(0, planes, depth):
+        for part in range(parts):
+            edges = stack_edges(first_ref, second_ref, part, start // GROUP)
+            blocks = []
+            for z in range(start, start + depth):
+                high, low = split(field_ref[part, z])
+                edge = jnp.where(row == z % GROUP, edges, 0.0).astype(BF16)
+                blocks.append(jnp.concatenate([high, low, high, edge]))
+            sums = jnp.dot(
+                main_ref[...], jnp.concatenate(blocks, axis=1), preferred_element_type=F32
             )
+            for z in range(start, start + depth):
+                piece = sums[:, (z - start) * rows : (z - start + 1) * rows]
+                out_ref[part, z] = field_ref[0, z] * piece[:rows] + piece[rows:] + add_ref[part, z]
+            place = pl.ds(start, depth)
+            copies.append(
+                pltpu.make_async_copy(
+                    out_ref.at[part, place], out_hbm.at[part, place], sems.at[len(copies)]
+                )
+            )
+            copies[-1].start()
+    for copy in copies:
+        copy.wait()
 
 
 def exchange(first, second, axis, count, periodic):
@@ -395,8 +413,10 @@
     return first, second
 
 
-CHUNK = 2
+CHUNK = 4
+X_CHUNK = 4
 DEPTH = 8
+OUT_DEPTH = 4
 
 
 def on_device(x_parts, y_parts, velocity, metric_first, metric_curve):
@@ -405,61 +425,69 @@
     y_sums, y_main, y_edge = y_tables(y_parts, rows)
     vmem = pl.BlockSpec(memory_space=pltpu.VMEM)
     outside = pl.BlockSpec(memory_space=pltpu.HBM)
-    edge_shape = jax.ShapeDtypeStruct((KINDS, parts, planes, rows), F32)
-
-    def on_chip(shape, dtype):
-        return pltpu.VMEM(shape, dtype)
-
-    in_specs = [outside] * 6
-    x1, x2, y1, y2, field, x_main, y_main, y_edge = pl.pallas_call(
-        functools.partial(edge_kernel, CHUNK),
-        out_shape=[edge_shape] * 4
-        + [
-            on_chip(velocity.shape, F32),
-            on_chip(x_main.shape[1:], BF16),
-            on_chip(y_main.shape[1:], F32),
-            on_chip(y_edge.shape[1:], F32),
+    edge_shape = (KINDS, parts, planes, rows)
+    params = pltpu.CompilerParams(vmem_limit_bytes=16 << 20)
+
+    y1, y2, field, x_sums_, x_main, y_main, y_edge = pl.pallas_call(
+        functools.partial(y_edge_kernel, CHUNK),
+        out_shape=[
+            pltpu.VMEM(edge_shape, F32),
+            pltpu.VMEM(edge_shape, F32),
+            pltpu.VMEM(velocity.shape, F32),
+            pltpu.VMEM(x_sums.shape, F32),
+            pltpu.VMEM(x_main.shape[1:], BF16),
+            pltpu.VMEM(y_main.shape[1:], F32),
+            pltpu.VMEM(y_edge.shape[1:], F32),
         ],
-        in_specs=in_specs,
-        out_specs=[vmem] * 8,
+        in_specs=[outside] * 6,
+        out_specs=[vmem] * 7,
         scratch_shapes=[
-            pltpu.VMEM(x_sums.shape[1:], BF16),
-            pltpu.VMEM(y_sums.shape[1:], BF16),
-            pltpu.VMEM((parts, EDGES, rows), F32),
+            pltpu.VMEM(y_sums.shape, BF16),
             pltpu.VMEM((parts, rows, rows), F32),
             pltpu.SemaphoreType.DMA((planes // CHUNK,)),
             pltpu.SemaphoreType.DMA((5,)),
         ],
-        compiler_params=pltpu.CompilerParams(vmem_limit_bytes=16 << 20),
-        name="edges",
+        compiler_params=params,
+        name="y_edges",
     )(*[
         pltpu.with_memory_space_constraint(item, pltpu.HBM)
-        for item in (velocity, x_sums, y_sums, x_main, y_main, y_edge)
+        for item in (velocity, y_sums, x_sums, x_main, y_main, y_edge)
     ])
-
     y1, y2 = exchange(y1, y2, "gy", y_parts, False)
+
+    x1, x2 = pl.pallas_call(
+        functools.partial(x_edge_kernel, X_CHUNK, spans_of(x_sums)),
+        out_shape=[pltpu.VMEM(edge_shape, F32)] * 2,
+        in_specs=[vmem] * 2,
+        out_specs=[vmem] * 2,
+        scratch_shapes=[pltpu.VMEM((2,) + edge_shape, F32)],
+        compiler_params=params,
+        name="x_edges",
+    )(field, x_sums_)
     x1, x2 = exchange(x1, x2, "gx", x_parts, True)
 
-    params = pltpu.CompilerParams(vmem_limit_bytes=16 << 20)
     partial = pl.pallas_call(
         functools.partial(wall_normal_kernel, DEPTH),
-        out_shape=on_chip(velocity.shape, F32),
+        out_shape=pltpu.VMEM(velocity.shape, F32),
         in_specs=[vmem] * 7,
         out_specs=vmem,
         scratch_shapes=[pltpu.VMEM((4 * rows, 2 * rows), BF16)],
         compiler_params=params,
         name="wall_normal",
-    )(field, y1, y2, y_main, y_edge, metric_first[None], metric_curve[None])
+    )(field, y2, y1, y_main, y_edge, metric_first[None], metric_curve[None])
 
     return pl.pallas_call(
-        functools.partial(streamwise_kernel, DEPTH),
+        functools.partial(streamwise_kernel, OUT_DEPTH),
         out_shape=jax.ShapeDtypeStruct(velocity.shape, F32),
-        grid=(planes // DEPTH,),
         in_specs=[vmem] * 5,
-        out_specs=pl.BlockSpec((parts, DEPTH, rows, rows), lambda i: (0, i, 0, 0)),
+        out_specs=outside,
+        scratch_shapes=[
+            pltpu.VMEM(velocity.shape, F32),
+            pltpu.SemaphoreType.DMA((parts * planes // OUT_DEPTH,)),
+        ],
         compiler_params=params,
         name="streamwise",
-    )(field, x1, x2, x_main, partial)
+    )(field, x2, x1, x_main, partial)
 
 
 def solution(mesh):

time: 23.4 us -> 20.7 us (0.88)
  Pallas kernels: 9.94 us -> 8.6 us
  starting transfers between devices: 10.8 us -> 9.53 us
    ppermute x2, waiting for transfers between devices: 2.44 us -> 1.04 us  [exchange(): lax.ppermute(second, axis, [p for a, b in pairs for p in ((a, b), (b, a))])]
    pallas_call x3 -> x4, Pallas kernels: 9.94 us -> 8.6 us  [the longest x1 2.94 us: on_device(): pl.pallas_call(functools.partial(y_edge_kernel, CHUNK), out_shape=[pltpu....]
    ppermute x2, starting transfers between devices: 9.99 us -> 8.75 us  [exchange(): lax.ppermute(second, axis, [p for a, b in pairs for p in ((a, b), (b, a))])]
    ppermute x2, waiting for transfers between devices: 0.01 us -> 1.19 us  [exchange(): lax.ppermute(first, axis, [p for a, b in pairs for p in ((a, b), (b, a))])]
  transfers between devices with their start and end apart: 4 -> 4, of which waited for: 1 -> 2; matrix products, arithmetic and copies ran while one was open for 0% -> 0% of each run, Pallas kernels for 9% -> 14%
where the time goes in v1:
time: 20.7 us; the launch traced here: 20.4 us
  starting transfers between devices  9.53 us (46%)
  Pallas kernels  8.6 us (42%)
  waiting for transfers between devices  2.23 us (11%)
    ppermute x2, starting transfers between devices, exchange(): lax.ppermute(second, axis, [p for a, b in pairs for p in ((a, b), (b, a))])  8.75 us
    pallas_call x1, Pallas kernels, on_device(): pl.pallas_call(functools.partial(y_edge_kernel, CHUNK), out_shape=[pltpu....  2.94 us
    pallas_call x1, Pallas kernels, on_device(): pl.pallas_call(functools.partial(streamwise_kernel, OUT_DEPTH), out_shape...  2.75 us
    pallas_call x1, Pallas kernels, on_device(): pl.pallas_call(functools.partial(wall_normal_kernel, DEPTH), out_shape=pl...  2.09 us
    ppermute x2, waiting for transfers between devices, exchange(): lax.ppermute(first, axis, [p for a, b in pairs for p in ((a, b), (b, a))])  1.19 us
    ppermute x2, waiting for transfers between devices, exchange(): lax.ppermute(second, axis, [p for a, b in pairs for p in ((a, b), (b, a))])  1.04 us
    pallas_call x1, Pallas kernels, on_device(): pl.pallas_call(functools.partial(x_edge_kernel, X_CHUNK, spans_of(x_sums)...  0.83 us
    ppermute x2, starting transfers between devices, exchange(): lax.ppermute(first, axis, [p for a, b in pairs for p in ((a, b), (b, a))])  0.78 us
  transfers between devices with their start and end apart: 4, of which 2 were waited for; matrix products, arithmetic and copies ran while one was open for 0% of the time, Pallas kernels for 14%

profile of v1, /device:TPU:2, one launch (start us, length us, event | category | flops | bytes accessed | tf_op | source)
XLA Modules:
  0.0 20.4 jit_solution(10934021433228701487)
XLA Ops:
  0.0 0.0 copy-start.1
  0.0 0.0 copy-start
  0.0 2.9 %y_edges.1 = (f32[3,3,16,128]{3,2,1,0:T(8,128)S(1)}, f32[3,3,16,128]{3,2,1,0:T(8,128)S(1)}, f32[3,16,128,128]{3,2,1,0:T(8,128)S(1)}, f32[4,128,128]{2,1,0:T(8,12...) custom-call(f32[3,16,128,128]{3,2,1,0:T(8,128)} %field_hbm.1, ...), custom_call_target="tpu_custom_call" | custom-call | tf_op jit(solution)/shard_map/y_edges/pallas_call | solution.py:431
  2.9 4.5 %collective-permute-start.2 = (f32[3,3,16,128]{3,2,1,0:T(8,128)S(1)}, f32[3,3,16,128]{3,2,1,0:T(8,128)S(1)}, u32[]{:S(2)}, u32[]{:S(2)}) collective-permute-start(f32[3,3,16,128]{3,2,1,0:T(8,128)S(1)} %get-tuple-element.19), channel_id=1, source_target_pairs={{1,2},{2,1},{3,4},{4,3},{5,6},{6,5},{7,8},{8,7},{9,10},{10,9},{11,... | collective-permute-start | bytes 221192 | tf_op jit(solution)/shard_map/ppermute | solution.py:412
  7.5 0.8 %collective-permute-start.3 = (f32[3,3,16,128]{3,2,1,0:T(8,128)S(1)}, f32[3,3,16,128]{3,2,1,0:T(8,128)S(1)}, u32[]{:S(2)}, u32[]{:S(2)}) collective-permute-start(f32[3,3,16,128]{3,2,1,0:T(8,128)S(1)} %get-tuple-element.20), channel_id=1, source_target_pairs={{0,1},{1,0},{2,3},{3,2},{4,5},{5,4},{6,7},{7,6},{8,9},{9,8},{10,11... | collective-permute-start | bytes 221192 | tf_op jit(solution)/shard_map/ppermute | solution.py:410
  8.3 0.8 %x_edges.1 = (f32[3,3,16,128]{3,2,1,0:T(8,128)S(1)}, f32[3,3,16,128]{3,2,1,0:T(8,128)S(1)}) custom-call(f32[3,16,128,128]{3,2,1,0:T(8,128)S(1)} %get-tuple-element.14.field_ref, f32[4,128,128]{2,1,0:T(8,128)S(1)} %get-tuple-element.15.x_ref), custom_call_target="tpu_custom_call" | custom-call | tf_op jit(solution)/shard_map/x_edges/pallas_call | solution.py:458
  9.1 4.2 %collective-permute-start = (f32[3,3,16,128]{3,2,1,0:T(8,128)S(1)}, f32[3,3,16,128]{3,2,1,0:T(8,128)S(1)}, u32[]{:S(2)}, u32[]{:S(2)}) collective-permute-start(f32[3,3,16,128]{3,2,1,0:T(8,128)S(1)} %get-tuple-element.16), channel_id=1, source_target_pairs={{16,32},{32,16},{48,64},{64,48},{80,96},{96,80},{112,0},{0,112},{1... | collective-permute-start | bytes 221192 | tf_op jit(solution)/shard_map/ppermute | solution.py:412
  13.3 0.0 collective-permute-start.1
  13.3 0.0 collective-permute-done.2.second_ref
  13.3 0.0 collective-permute-done.3.first_ref
  13.3 0.0 copy-done.1
  13.3 0.0 copy-done
  13.4 2.1 %wall_normal.1.add_ref = f32[3,16,128,128]{3,2,1,0:T(8,128)S(1)} custom-call(f32[3,16,128,128]{3,2,1,0:T(8,128)S(1)} %get-tuple-element.14.field_ref, f32[3,3,16,128]{3,2,1,0:T(8,128)S(1)} %collective-permute-done.2.second_ref, f32[3,3,16,128]{3,2,1,0:T(8,128)S(1)} %collective-permute-done.3.first_ref, f32[128,256]{1,0:T(8,128)S(1)} %get-tuple-element.21.main_ref, ...), custom_call_target="tpu_custom_call" | custom-call | tf_op jit(solution)/shard_map/wall_normal/pallas_call | solution.py:469
  15.5 1.0 %collective-permute-done.second_ref = f32[3,3,16,128]{3,2,1,0:T(8,128)S(1)} collective-permute-done((f32[3,3,16,128]{3,2,1,0:T(8,128)S(1)}, f32[3,3,16,128]{3,2,1,0:T(8,128)S(1)}, u32[]{:S(2)}, u32[]{:S(2)}) %collective-permute-start) | collective-permute-done | bytes 73760 | tf_op jit(solution)/shard_map/ppermute | solution.py:412
  16.5 1.2 %collective-permute-done.1.first_ref = f32[3,3,16,128]{3,2,1,0:T(8,128)S(1)} collective-permute-done((f32[3,3,16,128]{3,2,1,0:T(8,128)S(1)}, f32[3,3,16,128]{3,2,1,0:T(8,128)S(1)}, u32[]{:S(2)}, u32[]{:S(2)}) %collective-permute-start.1) | collective-permute-done | bytes 73760 | tf_op jit(solution)/shard_map/ppermute | solution.py:410
  17.7 2.7 %streamwise.1 = f32[3,16,128,128]{3,2,1,0:T(8,128)} custom-call(f32[3,16,128,128]{3,2,1,0:T(8,128)S(1)} %get-tuple-element.14.field_ref, f32[3,3,16,128]{3,2,1,0:T(8,128)S(1)} %collective-permute-done.second_ref, f32[3,3,16,128]{3,2,1,0:T(8,128)S(1)} %collective-permute-done.1.first_ref, bf16[256,512]{1,0:T(8,128)(2,1)S(1)} %get-tuple-element.18.main_ref, ...), custom_call_target="tpu_custom_call" | custom-call | tf_op jit(solution)/shard_map/streamwise/pallas_call | solution.py:479
Async XLA Ops:
  0.0 13.3 %copy-start.1 = (f32[128]{0:T(128)S(1)}, f32[128]{0:T(128)}, u32[]{:S(2)}) copy-start(f32[128]{0:T(128)} %param.10) | copy-start | bytes 1540
  0.0 13.3 %copy-start = (f32[128]{0:T(128)S(1)}, f32[128]{0:T(128)}, u32[]{:S(2)}) copy-start(f32[128]{0:T(128)} %param.9) | copy-start | bytes 1540
  2.9 10.4 %collective-permute-start.2 = (f32[3,3,16,128]{3,2,1,0:T(8,128)S(1)}, f32[3,3,16,128]{3,2,1,0:T(8,128)S(1)}, u32[]{:S(2)}, u32[]{:S(2)}) collective-permute-start(f32[3,3,16,128]{3,2,1,0:T(8,128)S(1)} %get-tuple-element.19), channel_id=1, source_target_pairs={{1,2},{2,1},{3,4},{4,3},{5,6},{6,5},{7,8},{8,7},{9,10},{10,9},{11,... | collective-permute-start | bytes 221192 | tf_op jit(solution)/shard_map/ppermute | solution.py:412
  7.5 5.9 %collective-permute-start.3 = (f32[3,3,16,128]{3,2,1,0:T(8,128)S(1)}, f32[3,3,16,128]{3,2,1,0:T(8,128)S(1)}, u32[]{:S(2)}, u32[]{:S(2)}) collective-permute-start(f32[3,3,16,128]{3,2,1,0:T(8,128)S(1)} %get-tuple-element.20), channel_id=1, source_target_pairs={{0,1},{1,0},{2,3},{3,2},{4,5},{5,4},{6,7},{7,6},{8,9},{9,8},{10,11... | collective-permute-start | bytes 221192 | tf_op jit(solution)/shard_map/ppermute | solution.py:410
  9.1 7.4 %collective-permute-start = (f32[3,3,16,128]{3,2,1,0:T(8,128)S(1)}, f32[3,3,16,128]{3,2,1,0:T(8,128)S(1)}, u32[]{:S(2)}, u32[]{:S(2)}) collective-permute-start(f32[3,3,16,128]{3,2,1,0:T(8,128)S(1)} %get-tuple-element.16), channel_id=1, source_target_pairs={{16,32},{32,16},{48,64},{64,48},{80,96},{96,80},{112,0},{0,112},{1... | collective-permute-start | bytes 221192 | tf_op jit(solution)/shard_map/ppermute | solution.py:412
  13.3 4.4 %collective-permute-start.1 = (f32[3,3,16,128]{3,2,1,0:T(8,128)S(1)}, f32[3,3,16,128]{3,2,1,0:T(8,128)S(1)}, u32[]{:S(2)}, u32[]{:S(2)}) collective-permute-start(f32[3,3,16,128]{3,2,1,0:T(8,128)S(1)} %get-tuple-element.17), channel_id=1, source_target_pairs={{0,16},{16,0},{32,48},{48,32},{64,80},{80,64},{96,112},{112,96},{1... | collective-permute-start | bytes 221192 | tf_op jit(solution)/shard_map/ppermute | solution.py:410
